TPU v7x, 32 devices: a whole 2x2x4 slice. The times are simulated.
32 devices in a mesh: groups: 2 (over x), ctx: 16 (over z, y, core).
Axes of the slice: x: 2, y: 2, z: 4, core: 2. Of those that a mesh axis runs over, the one named last changes fastest.
Arguments:
- queries: bfloat16 [8192, 2560], P(('groups', 'ctx')), parts along dimension 0, may hold values from -6 to 6
- keys: bfloat16 [8192, 2560], P(('groups', 'ctx')), parts along dimension 0, may hold values from -6 to 6
- values: bfloat16 [8192, 2560], P(('groups', 'ctx')), parts along dimension 0, may hold values from -6 to 6
- kv_lists: int32 [16, 4, 2, 8], P('ctx'), may hold values from 0 to 7, as said below
- kv_counts: int32 [16, 4, 2], P('ctx'), may hold values from 0 to 8, as said below
Outputs:
- attended: bfloat16 [8192, 2560], P(('groups', 'ctx')), parts along dimension 0
There are 2 independent parts, one for each index of `groups`. A program takes and returns all parts, laid end to end along the dimension named above; an argument that names none is the same for every part. Nothing has to cross between parts.
Inputs may be any that keep to these rules, and one draw needn't show every extreme that they name: For every device d, level k and side s, the first 8 // 2**k entries of kv_lists[d, k, s] are distinct block indices; later entries are never read. kv_counts[d, k, s] is at most 8 // 2**k and reaches it for some device at every level and side; it is 0 exactly where the partner d - 2**k (s = 0) or d + 2**k (s = 1) lies outside 0 to 15, else 1 or more.
All inputs are finite; a program needn't handle non-finite values.
Results may differ from a plain program's by a relative error of at most 0.005.
Values may be sent and summed in bfloat16 or wider, within the bound.
A program may use at most 128 MiB of HBM per device.

v0:
```python
import math
import jax
import jax.numpy as jnp
from jax import lax
from jax.sharding import PartitionSpec as P

HEAD = 128
masked_score = -1e30


def from_behind(block, axis, distance):
    devices = range(lax.axis_size(axis))
    route = [(i - distance, i) for i in devices if i - distance in devices]
    return lax.ppermute(block, axis, route)


def attend(carried, query_heads, key_rows, value_rows, allowed):
    best_score, weight_total, weighted = carried
    head_count = query_heads.shape[1]
    head_size = query_heads.shape[2]
    key_heads = key_rows.reshape(key_rows.shape[0], head_count, head_size)
    value_heads = value_rows.reshape(value_rows.shape[0], head_count, head_size)
    scores = jnp.einsum(
        "qhd,khd->hqk", query_heads, key_heads, preferred_element_type=jnp.float32
    ) * (1.0 / math.sqrt(head_size))
    if allowed is not None:
        scores = jnp.where(allowed[None, None, :], scores, masked_score)
    fresh_best = jnp.maximum(best_score, jnp.max(scores, axis=-1))
    weights = jnp.exp(scores - fresh_best[:, :, None])
    factor = jnp.exp(best_score - fresh_best)
    weight_total = weight_total * factor + jnp.sum(weights, axis=-1)
    mixed_values = jnp.einsum(
        "hqk,khd->qhd",
        weights.astype(jnp.bfloat16),
        value_heads,
        preferred_element_type=jnp.float32,
    )
    weighted = weighted * jnp.transpose(factor)[:, :, None] + mixed_values
    return (fresh_best, weight_total, weighted)


def shards(queries, keys, values, kv_lists, kv_counts):
    row_count = queries.shape[0]
    width = queries.shape[1]
    head_count = width // HEAD
    block_count = kv_lists.shape[3]
    level_count = kv_lists.shape[1]
    block_rows = row_count // block_count
    query_heads = queries.reshape(row_count, head_count, HEAD)
    carried = (
        jnp.full((head_count, row_count), masked_score, jnp.float32),
        jnp.zeros((head_count, row_count), jnp.float32),
        jnp.zeros((row_count, head_count, HEAD), jnp.float32),
    )
    carried = attend(carried, query_heads, keys, values, None)
    key_blocks = keys.reshape(block_count, block_rows, width)
    value_blocks = values.reshape(block_count, block_rows, width)
    every_list = lax.all_gather(kv_lists, "ctx", axis=0, tiled=True)
    here_index = lax.axis_index("ctx")
    ctx_count = lax.axis_size("ctx")
    for level_id in range(level_count):
        distance = 1 << level_id
        capacity = block_count >> level_id
        for side_id in range(2):
            offset = distance if side_id == 0 else -distance
            counted = kv_counts[0, level_id, side_id]
            allowed = jnp.arange(capacity * block_rows, dtype=jnp.int32) // block_rows < counted
            target = jnp.clip(here_index + offset, 0, ctx_count - 1)
            wanted = lax.dynamic_index_in_dim(every_list, target, 0, keepdims=False)[
                level_id, side_id, :capacity
            ]
            packed = jnp.stack(
                [jnp.take(key_blocks, wanted, axis=0), jnp.take(value_blocks, wanted, axis=0)]
            )
            arrived = from_behind(packed, "ctx", offset)
            far_keys = arrived[0]
            far_values = arrived[1]
            carried = attend(
                carried,
                query_heads,
                far_keys.reshape(capacity * block_rows, width),
                far_values.reshape(capacity * block_rows, width),
                allowed,
            )
    best_score, weight_total, weighted = carried
    result = weighted / jnp.transpose(weight_total)[:, :, None]
    return result.reshape(row_count, width).astype(jnp.bfloat16)


def solution(mesh):
    in_specs = (
        P(("groups", "ctx"), None),
        P(("groups", "ctx"), None),
        P(("groups", "ctx"), None),
        P("ctx", None, None, None),
        P("ctx", None, None),
    )
    out_specs = P(("groups", "ctx"), None)
    return jax.shard_map(shards, mesh=mesh, in_specs=in_specs, out_specs=out_specs, check_vma=False)
```

profile of v0, /device:TPU:10, one launch (start us, length us, event | category | flops | bytes accessed | tf_op | source)
XLA Modules:
  0.0 219.9 jit_solution(879587065999367864)
XLA Ops:
  0.8 19.0 %all_gather.3 = s32[16,4,2,8]{3,1,2,0:T(4,128)S(1)} all-gather(s32[1,4,2,8]{3,1,2,0:T(4,128)S(1)} %copy.64), channel_id=1, replica_groups=mesh['groups'=2,'ctx'=16] {'ctx'}, dimensions={0}, use_global_device_ids=true | all-gather | bytes 4352 | tf_op jit(solution)/shard_map/all_gather | solution.py:58
  26.8 2.4 %collective-permute-start.1 = (bf16[2,8,32,2560]{3,2,1,0:T(8,128)(2,1)}, bf16[2,8,32,2560]{3,2,1,0:T(8,128)(2,1)}, u32[]{:S(2)}, u32[]{:S(2)}) collective-permute-start(bf16[2,8,32,2560]{3,2,1,0:T(8,128)(2,1)} %pad_maximum_fusion.1), channel_id=1, source_target_pairs={{1,0},{2,1},{3,2},{4,3},{5,4},{6,5},{7,6},{8,7},{9,8},{10,9},{11,1... | collective-permute-start | bytes 7864328 | tf_op jit(solution)/shard_map/ppermute | solution.py:14
  42.9 6.1 %collective-permute-start.3 = (bf16[2,4,32,2560]{3,2,1,0:T(8,128)(2,1)}, bf16[2,4,32,2560]{3,2,1,0:T(8,128)(2,1)}, u32[]{:S(2)}, u32[]{:S(2)}) collective-permute-start(bf16[2,4,32,2560]{3,2,1,0:T(8,128)(2,1)} %pad_maximum_fusion.3), channel_id=1, source_target_pairs={{2,0},{3,1},{4,2},{5,3},{6,4},{7,5},{8,6},{9,7},{10,8},{11,9},{12,... | collective-permute-start | bytes 3932168 | tf_op jit(solution)/shard_map/ppermute | solution.py:14
  79.9 3.2 %multiply_reduce_fusion = (f32[20,256]{1,0:T(8,128)S(1)}, f32[20,256,256]{1,2,0:T(8,128)}) fusion(bf16[256,20,128]{0,2,1:T(8,128)(2,1)S(1)} %bitcast.392, bf16[256,20,128]{0,2,1:T(8,128)(2,1)S(1)} %bitcast.417), kind=kOutput, calls=%fused_computation.21 | convolution fusion | flops 338160640 | bytes 7884800 | tf_op jit(solution)/shard_map/qhd,khd->hqk/dot_general | solution.py:23
  83.2 11.3 %collective-permute-done.7 = bf16[2,1,32,2560]{3,2,1,0:T(8,128)(2,1)} collective-permute-done((bf16[2,1,32,2560]{3,2,1,0:T(8,128)(2,1)}, bf16[2,1,32,2560]{3,2,1,0:T(8,128)(2,1)}, u32[]{:S(2)}, u32[]{:S(2)}) %collective-permute-start.7) | collective-permute-done | bytes 327712 | tf_op jit(solution)/shard_map/ppermute | solution.py:14
  96.9 3.5 %collective-permute-done.6 = bf16[2,1,32,2560]{3,2,1,0:T(8,128)(2,1)S(1)} collective-permute-done((bf16[2,1,32,2560]{3,2,1,0:T(8,128)(2,1)S(1)}, bf16[2,1,32,2560]{3,2,1,0:T(8,128)(2,1)S(1)}, u32[]{:S(2)}, u32[]{:S(2)}) %collective-permute-start.6) | collective-permute-done | bytes 327712 | tf_op jit(solution)/shard_map/ppermute | solution.py:14
  100.5 9.0 %collective-permute-start.5 = (bf16[2,2,32,2560]{3,2,1,0:T(8,128)(2,1)}, bf16[2,2,32,2560]{3,2,1,0:T(8,128)(2,1)}, u32[]{:S(2)}, u32[]{:S(2)}) collective-permute-start(bf16[2,2,32,2560]{3,2,1,0:T(8,128)(2,1)} %pad_maximum_fusion.5), channel_id=1, source_target_pairs={{4,0},{5,1},{6,2},{7,3},{8,4},{9,5},{10,6},{11,7},{12,8},{13,9},{1... | collective-permute-start | bytes 1966088 | tf_op jit(solution)/shard_map/ppermute | solution.py:14
  113.4 6.9 %collective-permute-done.5 = bf16[2,2,32,2560]{3,2,1,0:T(8,128)(2,1)} collective-permute-done((bf16[2,2,32,2560]{3,2,1,0:T(8,128)(2,1)}, bf16[2,2,32,2560]{3,2,1,0:T(8,128)(2,1)}, u32[]{:S(2)}, u32[]{:S(2)}) %collective-permute-start.5) | collective-permute-done | bytes 655392 | tf_op jit(solution)/shard_map/ppermute | solution.py:14
  120.3 3.9 %collective-permute-start.4 = (bf16[2,2,32,2560]{3,2,1,0:T(8,128)(2,1)}, bf16[2,2,32,2560]{3,2,1,0:T(8,128)(2,1)}, u32[]{:S(2)}, u32[]{:S(2)}) collective-permute-start(bf16[2,2,32,2560]{3,2,1,0:T(8,128)(2,1)} %pad_maximum_fusion.4), channel_id=1, source_target_pairs={{0,4},{1,5},{2,6},{3,7},{4,8},{5,9},{6,10},{7,11},{8,12},{9,13},{1... | collective-permute-start | bytes 1966088 | tf_op jit(solution)/shard_map/ppermute | solution.py:14
  126.3 6.8 %collective-permute-done.4 = bf16[2,2,32,2560]{3,2,1,0:T(8,128)(2,1)} collective-permute-done((bf16[2,2,32,2560]{3,2,1,0:T(8,128)(2,1)}, bf16[2,2,32,2560]{3,2,1,0:T(8,128)(2,1)}, u32[]{:S(2)}, u32[]{:S(2)}) %collective-permute-start.4) | collective-permute-done | bytes 655392 | tf_op jit(solution)/shard_map/ppermute | solution.py:14
  137.0 2.0 fusion.135
  139.1 2.0 fusion.136
  141.1 3.8 %collective-permute-done.3 = bf16[2,4,32,2560]{3,2,1,0:T(8,128)(2,1)} collective-permute-done((bf16[2,4,32,2560]{3,2,1,0:T(8,128)(2,1)}, bf16[2,4,32,2560]{3,2,1,0:T(8,128)(2,1)}, u32[]{:S(2)}, u32[]{:S(2)}) %collective-permute-start.3) | collective-permute-done | bytes 1310752 | tf_op jit(solution)/shard_map/ppermute | solution.py:14
  144.9 2.5 %fusion.127 = (bf16[1,4,32,2560]{3,2,1,0:T(8,128)(2,1)}, bf16[1,4,32,2560]{3,2,1,0:T(8,128)(2,1)}) fusion(bf16[2,4,32,2560]{3,2,1,0:T(8,128)(2,1)} %collective-permute-done.3), kind=kLoop, calls=%fused_computation.273 | loop fusion | bytes 2621440 | tf_op jit(solution)/shard_map/slice | solution.py:77
  147.4 2.3 %reshape_reshape_squeeze.54 = bf16[128,20,128]{2,1,0:T(8,128)(2,1)} reshape(bf16[1,4,32,2560]{3,2,1,0:T(8,128)(2,1)} %get-tuple-element.57) | data formatting | bytes 1310720 | tf_op jit(solution)/shard_map/reshape;reshape;squeeze | solution.py:21
  149.7 2.5 %fusion.126 = (bf16[1,4,32,2560]{3,2,1,0:T(8,128)(2,1)}, bf16[1,4,32,2560]{3,2,1,0:T(8,128)(2,1)}) fusion(bf16[2,4,32,2560]{3,2,1,0:T(8,128)(2,1)} %collective-permute-done.2), kind=kLoop, calls=%fused_computation.272 | loop fusion | bytes 2621440 | tf_op jit(solution)/shard_map/slice | solution.py:77
  152.1 2.2 %reshape_reshape_squeeze.52 = bf16[128,20,128]{2,1,0:T(8,128)(2,1)} reshape(bf16[1,4,32,2560]{3,2,1,0:T(8,128)(2,1)} %get-tuple-element.55) | data formatting | bytes 1310720 | tf_op jit(solution)/shard_map/reshape;reshape;squeeze | solution.py:21
  154.4 2.2 %reshape_reshape_squeeze.53 = bf16[128,20,128]{2,1,0:T(8,128)(2,1)} reshape(bf16[1,4,32,2560]{3,2,1,0:T(8,128)(2,1)} %get-tuple-element.54) | data formatting | bytes 1310720 | tf_op jit(solution)/shard_map/reshape;reshape;squeeze | solution.py:22
  156.6 2.2 %reshape_reshape_squeeze.55 = bf16[128,20,128]{2,1,0:T(8,128)(2,1)} reshape(bf16[1,4,32,2560]{3,2,1,0:T(8,128)(2,1)} %get-tuple-element.56) | data formatting | bytes 1310720 | tf_op jit(solution)/shard_map/reshape;reshape;squeeze | solution.py:22
  158.8 3.9 %bitcast_reduce_fusion.2 = (f32[20,256]{1,0:T(8,128)}, f32[20,128,256]{2,1,0:T(8,128)}) fusion(pred[128]{0:T(512)(128)(4,1)S(1)} %get-tuple-element.131, bf16[256,20,128]{0,2,1:T(8,128)(2,1)S(1)} %bitcast.397, bf16[128,20,128]{2,1,0:T(8,128)(2,1)} %reshape_reshape_squeeze.54), kind=kOutput, calls=%fused_computation.45 | convolution fusion | flops 169733120 | bytes 4608128 | tf_op jit(solution)/shard_map/qhd,khd->hqk/dot_general | solution.py:23
  162.7 2.1 bitcast_reduce_fusion.3
  164.8 3.5 %fusion.125 = (bf16[1,8,32,2560]{3,2,1,0:T(8,128)(2,1)}, bf16[1,8,32,2560]{3,2,1,0:T(8,128)(2,1)}) fusion(bf16[2,8,32,2560]{3,2,1,0:T(8,128)(2,1)} %collective-permute-done.1), kind=kLoop, calls=%fused_computation.271 | loop fusion | bytes 5242880 | tf_op jit(solution)/shard_map/slice | solution.py:77
  168.3 3.5 %reshape_reshape_squeeze.50 = bf16[256,20,128]{2,1,0:T(8,128)(2,1)} reshape(bf16[1,8,32,2560]{3,2,1,0:T(8,128)(2,1)} %get-tuple-element.53) | data formatting | bytes 2621440 | tf_op jit(solution)/shard_map/reshape;reshape;squeeze | solution.py:21
  171.8 3.5 %fusion.124 = (bf16[1,8,32,2560]{3,2,1,0:T(8,128)(2,1)}, bf16[1,8,32,2560]{3,2,1,0:T(8,128)(2,1)}) fusion(bf16[2,8,32,2560]{3,2,1,0:T(8,128)(2,1)} %collective-permute-done), kind=kLoop, calls=%fused_computation.270 | loop fusion | bytes 5242880 | tf_op jit(solution)/shard_map/slice | solution.py:77
  175.3 3.5 %reshape_reshape_squeeze.48 = bf16[256,20,128]{2,1,0:T(8,128)(2,1)} reshape(bf16[1,8,32,2560]{3,2,1,0:T(8,128)(2,1)} %get-tuple-element.51) | data formatting | bytes 2621440 | tf_op jit(solution)/shard_map/reshape;reshape;squeeze | solution.py:21
  178.8 3.5 %reshape_reshape_squeeze.49 = bf16[256,20,128]{2,1,0:T(8,128)(2,1)} reshape(bf16[1,8,32,2560]{3,2,1,0:T(8,128)(2,1)} %get-tuple-element.50) | data formatting | bytes 2621440 | tf_op jit(solution)/shard_map/reshape;reshape;squeeze | solution.py:22
  182.3 5.2 %bitcast_reduce_fusion = (f32[20,256]{1,0:T(8,128)S(1)}, f32[20,256,256]{1,2,0:T(8,128)}) fusion(pred[256]{0:T(512)(128)(4,1)S(1)} %get-tuple-element.125, bf16[256,20,128]{0,2,1:T(8,128)(2,1)S(1)} %bitcast.399, bf16[256,20,128]{2,1,0:T(8,128)(2,1)} %reshape_reshape_squeeze.50), kind=kOutput, calls=%fused_computation.13 | convolution fusion | flops 339471360 | bytes 7885056 | tf_op jit(solution)/shard_map/qhd,khd->hqk/dot_general | solution.py:23
  190.6 2.4 %fusion.4 = f32[20,256]{1,0:T(8,128)} fusion(f32[20,256,256]{1,2,0:T(8,128)S(1)} %get-tuple-element.116, f32[20,256]{1,0:T(8,128)S(1)} %get-tuple-element.37, pred[256]{0:T(512)(128)(4,1)S(1)} %copy-done.48), kind=kLoop, calls=%fused_computation.24 | loop fusion | flops 5237760 | bytes 5284096 | tf_op jit(solution)/shard_map/reduce_sum | solution.py:31
  193.0 3.0 %fusion.10 = f32[20,128,256]{2,1,0:T(8,128)} fusion(f32[20,256,256]{1,2,0:T(8,128)S(1)} %get-tuple-element.116, f32[20,256]{1,0:T(8,128)S(1)} %get-tuple-element.37, pred[256]{0:T(512)(128)(4,1)S(1)} %copy-done.48, bf16[256,20,128]{2,1,0:T(8,128)(2,1)S(1)} %copy-done.8), kind=kOutput, calls=%fused_computation.29 | convolution fusion | flops 340787200 | bytes 9195776 | tf_op jit(solution)/shard_map/hqk,khd->qhd/dot_general | solution.py:32
  197.7 3.7 %fusion.6 = f32[20,256]{1,0:T(8,128)S(1)} fusion(f32[20,256,256]{1,2,0:T(8,128)} %get-tuple-element.114, f32[20,256]{1,0:T(8,128)} %get-tuple-element.36, pred[256]{0:T(512)(128)(4,1)} %copy-done.46), kind=kLoop, calls=%fused_computation.26 | loop fusion | flops 5237760 | bytes 5284096 | tf_op jit(solution)/shard_map/reduce_sum | solution.py:31
  201.4 3.9 %fusion.8 = f32[20,128,256]{2,1,0:T(8,128)S(1)} fusion(f32[20,256,256]{1,2,0:T(8,128)} %get-tuple-element.114, f32[20,256]{1,0:T(8,128)S(1)} %copy-done.38, pred[256]{0:T(512)(128)(4,1)S(1)} %copy-done.47, bf16[256,20,128]{2,1,0:T(8,128)(2,1)S(1)} %copy-done.9), kind=kOutput, calls=%fused_computation.28 | convolution fusion | flops 340787200 | bytes 9195776 | tf_op jit(solution)/shard_map/hqk,khd->qhd/dot_general | solution.py:32
  216.1 2.2 fusion.15
  (199 shorter events, 77.2 us)
Async XLA Ops:
  0.0 21.8 %copy-start.1 = (bf16[256,2560]{1,0:T(8,128)(2,1)S(1)}, bf16[256,2560]{1,0:T(8,128)(2,1)}, u32[]{:S(2)}) copy-start(bf16[256,2560]{1,0:T(8,128)(2,1)} %param.15) | copy-start | bytes 3932164
  25.1 4.1 %copy-start = (bf16[256,2560]{1,0:T(8,128)(2,1)S(1)}, bf16[256,2560]{1,0:T(8,128)(2,1)}, u32[]{:S(2)}) copy-start(bf16[256,2560]{1,0:T(8,128)(2,1)} %param.14) | copy-start | bytes 3932164
  26.8 137.9 %collective-permute-start.1 = (bf16[2,8,32,2560]{3,2,1,0:T(8,128)(2,1)}, bf16[2,8,32,2560]{3,2,1,0:T(8,128)(2,1)}, u32[]{:S(2)}, u32[]{:S(2)}) collective-permute-start(bf16[2,8,32,2560]{3,2,1,0:T(8,128)(2,1)} %pad_maximum_fusion.1), channel_id=1, source_target_pairs={{1,0},{2,1},{3,2},{4,3},{5,4},{6,5},{7,6},{8,7},{9,8},{10,9},{11,1... | collective-permute-start | bytes 7864328 | tf_op jit(solution)/shard_map/ppermute | solution.py:14
  36.5 135.4 %collective-permute-start = (bf16[2,8,32,2560]{3,2,1,0:T(8,128)(2,1)}, bf16[2,8,32,2560]{3,2,1,0:T(8,128)(2,1)}, u32[]{:S(2)}, u32[]{:S(2)}) collective-permute-start(bf16[2,8,32,2560]{3,2,1,0:T(8,128)(2,1)} %pad_maximum_fusion), channel_id=1, source_target_pairs={{0,1},{1,2},{2,3},{3,4},{4,5},{5,6},{6,7},{7,8},{8,9},{9,10},{10,1... | collective-permute-start | bytes 7864328 | tf_op jit(solution)/shard_map/ppermute | solution.py:14
  42.9 102.0 %collective-permute-start.3 = (bf16[2,4,32,2560]{3,2,1,0:T(8,128)(2,1)}, bf16[2,4,32,2560]{3,2,1,0:T(8,128)(2,1)}, u32[]{:S(2)}, u32[]{:S(2)}) collective-permute-start(bf16[2,4,32,2560]{3,2,1,0:T(8,128)(2,1)} %pad_maximum_fusion.3), channel_id=1, source_target_pairs={{2,0},{3,1},{4,2},{5,3},{6,4},{7,5},{8,6},{9,7},{10,8},{11,9},{12,... | collective-permute-start | bytes 3932168 | tf_op jit(solution)/shard_map/ppermute | solution.py:14
  53.5 96.1 %collective-permute-start.2 = (bf16[2,4,32,2560]{3,2,1,0:T(8,128)(2,1)}, bf16[2,4,32,2560]{3,2,1,0:T(8,128)(2,1)}, u32[]{:S(2)}, u32[]{:S(2)}) collective-permute-start(bf16[2,4,32,2560]{3,2,1,0:T(8,128)(2,1)} %pad_maximum_fusion.2), channel_id=1, source_target_pairs={{0,2},{1,3},{2,4},{3,5},{4,6},{5,7},{6,8},{7,9},{8,10},{9,11},{10,... | collective-permute-start | bytes 3932168 | tf_op jit(solution)/shard_map/ppermute | solution.py:14
  62.0 32.5 %collective-permute-start.7 = (bf16[2,1,32,2560]{3,2,1,0:T(8,128)(2,1)}, bf16[2,1,32,2560]{3,2,1,0:T(8,128)(2,1)}, u32[]{:S(2)}, u32[]{:S(2)}) collective-permute-start(bf16[2,1,32,2560]{3,2,1,0:T(8,128)(2,1)} %pad_maximum_fusion.7), channel_id=1, source_target_pairs={{8,0},{9,1},{10,2},{11,3},{12,4},{13,5},{14,6},{15,7},{24,16},{25,... | collective-permute-start | bytes 983048 | tf_op jit(solution)/shard_map/ppermute | solution.py:14
  67.1 2.9 %copy-start.45 = (s32[1,4,2]{1,2,0:T(2,128)S(1)}, s32[1,4,2]{1,2,0:T(2,128)}, u32[]{:S(2)}) copy-start(s32[1,4,2]{1,2,0:T(2,128)} %param.17) | copy-start | bytes 100
  70.0 5.3 %copy-start.19 = (bf16[2,32,2560]{2,1,0:T(8,128)(2,1)S(1)}, bf16[2,32,2560]{2,1,0:T(8,128)(2,1)}, u32[]{:S(2)}) copy-start(bf16[2,32,2560]{2,1,0:T(8,128)(2,1)} %gather_fusion.10) | copy-start | bytes 983044
  70.0 5.3 %copy-start.20 = (bf16[2,32,2560]{2,1,0:T(8,128)(2,1)S(1)}, bf16[2,32,2560]{2,1,0:T(8,128)(2,1)}, u32[]{:S(2)}) copy-start(bf16[2,32,2560]{2,1,0:T(8,128)(2,1)} %gather_fusion.11) | copy-start | bytes 983044
  74.0 108.3 %copy-start.46 = (pred[256]{0:T(512)(128)(4,1)}, pred[256]{0:T(512)(128)(4,1)S(1)}, u32[]{:S(2)}) copy-start(pred[256]{0:T(512)(128)(4,1)S(1)} %get-tuple-element.125) | copy-start | bytes 772
  75.3 4.6 %copy-start.11 = (bf16[256,2560]{0,1:T(8,128)(2,1)S(1)}, bf16[256,2560]{0,1:T(8,128)(2,1)}, u32[]{:S(2)}) copy-start(bf16[256,2560]{0,1:T(8,128)(2,1)} %copy.59) | copy-start | bytes 3932164
  79.9 3.2 %copy-start.22 = (bf16[1,1,32,2560]{3,2,1,0:T(8,128)(2,1)S(1)}, bf16[1,1,32,2560]{3,2,1,0:T(8,128)(2,1)}, u32[]{:S(2)}) copy-start(bf16[1,1,32,2560]{3,2,1,0:T(8,128)(2,1)} %get-tuple-element.61) | copy-start | bytes 491524
  94.5 6.0 %collective-permute-start.6 = (bf16[2,1,32,2560]{3,2,1,0:T(8,128)(2,1)S(1)}, bf16[2,1,32,2560]{3,2,1,0:T(8,128)(2,1)S(1)}, u32[]{:S(2)}, u32[]{:S(2)}) collective-permute-start(bf16[2,1,32,2560]{3,2,1,0:T(8,128)(2,1)S(1)} %pad_maximum_fusion.6), channel_id=1, source_target_pairs={{0,8},{1,9},{2,10},{3,11},{4,12},{5,13},{6,14},{7,15},{16,24},{17,... | collective-permute-start | bytes 983048 | tf_op jit(solution)/shard_map/ppermute | solution.py:14
  100.5 19.8 %collective-permute-start.5 = (bf16[2,2,32,2560]{3,2,1,0:T(8,128)(2,1)}, bf16[2,2,32,2560]{3,2,1,0:T(8,128)(2,1)}, u32[]{:S(2)}, u32[]{:S(2)}) collective-permute-start(bf16[2,2,32,2560]{3,2,1,0:T(8,128)(2,1)} %pad_maximum_fusion.5), channel_id=1, source_target_pairs={{4,0},{5,1},{6,2},{7,3},{8,4},{9,5},{10,6},{11,7},{12,8},{13,9},{1... | collective-permute-start | bytes 1966088 | tf_op jit(solution)/shard_map/ppermute | solution.py:14
  120.3 12.8 %collective-permute-start.4 = (bf16[2,2,32,2560]{3,2,1,0:T(8,128)(2,1)}, bf16[2,2,32,2560]{3,2,1,0:T(8,128)(2,1)}, u32[]{:S(2)}, u32[]{:S(2)}) collective-permute-start(bf16[2,2,32,2560]{3,2,1,0:T(8,128)(2,1)} %pad_maximum_fusion.4), channel_id=1, source_target_pairs={{0,4},{1,5},{2,6},{3,7},{4,8},{5,9},{6,10},{7,11},{8,12},{9,13},{1... | collective-permute-start | bytes 1966088 | tf_op jit(solution)/shard_map/ppermute | solution.py:14
  158.8 3.9 %copy-start.15 = (bf16[128,20,128]{2,1,0:T(8,128)(2,1)S(1)}, bf16[128,20,128]{2,1,0:T(8,128)(2,1)}, u32[]{:S(2)}) copy-start(bf16[128,20,128]{2,1,0:T(8,128)(2,1)} %reshape_reshape_squeeze.52) | copy-start | bytes 1966084
  182.3 5.2 %copy-start.7 = (bf16[256,20,128]{2,1,0:T(8,128)(2,1)S(1)}, bf16[256,20,128]{2,1,0:T(8,128)(2,1)}, u32[]{:S(2)}) copy-start(bf16[256,20,128]{2,1,0:T(8,128)(2,1)} %reshape_reshape_squeeze.48) | copy-start | bytes 3932164
  182.3 5.2 %copy-start.48 = (pred[256]{0:T(512)(128)(4,1)S(1)}, pred[256]{0:T(512)(128)(4,1)}, u32[]{:S(2)}) copy-start(pred[256]{0:T(512)(128)(4,1)} %get-tuple-element.126) | copy-start | bytes 772
  187.5 2.3 %copy-start.25 = (f32[20,256]{1,0:T(8,128)S(1)}, f32[20,256]{1,0:T(8,128)}, u32[]{:S(2)}) copy-start(f32[20,256]{1,0:T(8,128)} %get-tuple-element.101) | copy-start | bytes 61444
  187.5 2.3 %copy-start.27 = (f32[20,256]{1,0:T(8,128)S(1)}, f32[20,256]{1,0:T(8,128)}, u32[]{:S(2)}) copy-start(f32[20,256]{1,0:T(8,128)} %get-tuple-element.103) | copy-start | bytes 61444
  187.5 2.3 %copy-start.29 = (f32[20,256]{1,0:T(8,128)S(1)}, f32[20,256]{1,0:T(8,128)}, u32[]{:S(2)}) copy-start(f32[20,256]{1,0:T(8,128)} %get-tuple-element.105) | copy-start | bytes 61444
  187.5 2.3 %copy-start.31 = (f32[20,256]{1,0:T(8,128)S(1)}, f32[20,256]{1,0:T(8,128)}, u32[]{:S(2)}) copy-start(f32[20,256]{1,0:T(8,128)} %get-tuple-element.107) | copy-start | bytes 61444
  190.6 2.4 %copy-start.8 = (bf16[256,20,128]{2,1,0:T(8,128)(2,1)S(1)}, bf16[256,20,128]{2,1,0:T(8,128)(2,1)}, u32[]{:S(2)}) copy-start(bf16[256,20,128]{2,1,0:T(8,128)(2,1)} %reshape_reshape_squeeze.49) | copy-start | bytes 3932164
  193.0 3.0 %copy-start.10 = (bf16[1,8,32,2560]{3,2,1,0:T(8,128)(2,1)S(1)}, bf16[1,8,32,2560]{3,2,1,0:T(8,128)(2,1)}, u32[]{:S(2)}) copy-start(bf16[1,8,32,2560]{3,2,1,0:T(8,128)(2,1)} %get-tuple-element.52) | copy-start | bytes 3932164
  197.7 3.7 %copy-start.9 = (bf16[256,20,128]{2,1,0:T(8,128)(2,1)S(1)}, bf16[256,20,128]{2,1,0:T(8,128)(2,1)}, u32[]{:S(2)}) copy-start(bf16[256,20,128]{2,1,0:T(8,128)(2,1)} %reshape_reshape_squeeze.51) | copy-start | bytes 3932164
  197.7 3.7 %copy-start.38 = (f32[20,256]{1,0:T(8,128)S(1)}, f32[20,256]{1,0:T(8,128)}, u32[]{:S(2)}) copy-start(f32[20,256]{1,0:T(8,128)} %get-tuple-element.36) | copy-start | bytes 61444
  197.7 3.7 %copy-start.47 = (pred[256]{0:T(512)(128)(4,1)S(1)}, pred[256]{0:T(512)(128)(4,1)}, u32[]{:S(2)}) copy-start(pred[256]{0:T(512)(128)(4,1)} %copy-done.46) | copy-start | bytes 772
  201.4 4.0 %copy-start.3 = (f32[20,128,256]{2,1,0:T(8,128)S(1)}, f32[20,128,256]{2,1,0:T(8,128)}, u32[]{:S(2)}) copy-start(f32[20,128,256]{2,1,0:T(8,128)} %get-tuple-element.112) | copy-start | bytes 7864324
  201.4 4.0 %copy-start.24 = (f32[20,256]{1,0:T(8,128)S(1)}, f32[20,256]{1,0:T(8,128)}, u32[]{:S(2)}) copy-start(f32[20,256]{1,0:T(8,128)} %get-tuple-element.35) | copy-start | bytes 61444
  206.5 3.2 %slice-start = ((s8[5242880]{0:T(1024)(128)(4,1)}), s8[4194304]{0:T(1024)(128)(4,1)S(1)}, s32[]{:S(2)}) async-start(s8[5242880]{0:T(1024)(128)(4,1)} %bitcast.401), calls=%async_computation | async-start | bytes 8388608
  207.4 2.3 %slice-start.1 = ((s8[5242880]{0:T(1024)(128)(4,1)}), s8[1048576]{0:T(1024)(128)(4,1)S(1)}, s32[]{:S(2)}) async-start(s8[5242880]{0:T(1024)(128)(4,1)} %bitcast.401), calls=%async_computation.1 | async-start | bytes 2097152
  (27 other events, 34.6 us)
where the time goes:
time: 221 us; the launch traced here: 220 us
  local copies, waits for them, and re-layouts  67.7 us (31%)
  matrix products  36.2 us (16%)
  waiting for transfers between devices  32.4 us (15%)
  other arithmetic  31.7 us (14%)
  starting transfers between devices  27.9 us (13%)
  blocking collectives  19 us (9%)
  between operations  4.86 us (2%)
    ppermute x8, waiting for transfers between devices, from_behind(): return lax.ppermute(block, axis, route)  32.4 us
    ppermute x8, starting transfers between devices, from_behind(): return lax.ppermute(block, axis, route)  27.9 us
    dot_general x9, matrix products, attend(): jnp.einsum('qhd,khd->hqk', query_heads, key_heads, preferred_element_type...  22.7 us
    all_gather x1, blocking collectives, shards(): every_list = lax.all_gather(kv_lists, 'ctx', axis=0, tiled=True)  19 us
    another operation x16, other arithmetic, shards(): jnp.stack([jnp.take(key_blocks, wanted, axis=0), jnp.take(value_blocks, w...  15.7 us
    slice x8, local copies, waits for them, and re-layouts, shards(): far_values = arrived[1]  15.3 us
    another operation x8, local copies, waits for them, and re-layouts, attend(): key_heads = key_rows.reshape(key_rows.shape[0], head_count, head_size)  13.6 us
    dot_general x9, matrix products, attend(): jnp.einsum('hqk,khd->qhd', weights.astype(jnp.bfloat16), value_heads, pre...  13.5 us
  transfers between devices with their start and end apart: 8, of which 5 were waited for; matrix products, arithmetic and copies ran while one was open for 37% of the time, Pallas kernels for 0%

commit v1 on v0

--- a/solution.py
+++ b/solution.py
@@ -55,7 +55,9 @@
     carried = attend(carried, query_heads, keys, values, None)
     key_blocks = keys.reshape(block_count, block_rows, width)
     value_blocks = values.reshape(block_count, block_rows, width)
-    every_list = lax.all_gather(kv_lists, "ctx", axis=0, tiled=True)
+    every_list = jnp.concatenate(
+        lax.all_to_all(jnp.stack([kv_lists] * lax.axis_size("ctx")), "ctx", 0, 0), axis=0
+    )
     here_index = lax.axis_index("ctx")
     ctx_count = lax.axis_size("ctx")
     for level_id in range(level_count):

time: 221 us -> 263 us (1.19)
  waiting for transfers between devices: 32.4 us -> 72.2 us
  blocking collectives: 19 us -> 0 us
  starting transfers between devices: 27.9 us -> 40.6 us
  local copies, waits for them, and re-layouts: 67.7 us -> 78.7 us
  other arithmetic: 31.7 us -> 27.5 us
    ppermute x8, waiting for transfers between devices: 32.4 us -> 72.2 us  [from_behind(): return lax.ppermute(block, axis, route)]
    all_gather x1 -> x0, blocking collectives: 19 us -> none  [shards(): every_list = lax.all_gather(kv_lists, 'ctx', axis=0, tiled=True)]
    gather x6, local copies, waits for them, and re-layouts: 6.68 us -> 16 us  [shards(): jnp.take(key_blocks, wanted, axis=0)]
    ppermute x8, starting transfers between devices: 27.9 us -> 34.3 us  [from_behind(): return lax.ppermute(block, axis, route)]
    all_to_all x0 -> x1, starting transfers between devices: none -> 6.3 us  [shards(): lax.all_to_all(jnp.stack([kv_lists] * lax.axis_size('ctx')), 'ctx', 0, 0)]
    another operation x16 -> x15, other arithmetic: 15.7 us -> 11 us  [shards(): jnp.stack([jnp.take(key_blocks, wanted, axis=0), jnp.take(value_blocks, w...]
    unnamed x106 -> x115, local copies, waits for them, and re-layouts: 8.28 us -> 7.56 us
  transfers between devices with their start and end apart: 8 -> 9, of which waited for: 5 -> 4; matrix products, arithmetic and copies ran while one was open for 37% -> 25% of each run, Pallas kernels for 0% -> 0%
where the time goes in v1:
time: 263 us; the launch traced here: 261 us
  local copies, waits for them, and re-layouts  78.7 us (30%)
  waiting for transfers between devices  72.2 us (27%)
  starting transfers between devices  40.6 us (15%)
  matrix products  37.7 us (14%)
  other arithmetic  27.5 us (10%)
  between operations  4.42 us (2%)
    ppermute x8, waiting for transfers between devices, from_behind(): return lax.ppermute(block, axis, route)  72.2 us
    ppermute x8, starting transfers between devices, from_behind(): return lax.ppermute(block, axis, route)  34.3 us
    dot_general x9, matrix products, attend(): jnp.einsum('qhd,khd->hqk', query_heads, key_heads, preferred_element_type...  24.2 us
    gather x6, local copies, waits for them, and re-layouts, shards(): jnp.take(key_blocks, wanted, axis=0)  16 us
    slice x8, local copies, waits for them, and re-layouts, shards(): far_values = arrived[1]  14.3 us
    another operation x8, local copies, waits for them, and re-layouts, attend(): key_heads = key_rows.reshape(key_rows.shape[0], head_count, head_size)  13.7 us
    dot_general x9, matrix products, attend(): jnp.einsum('hqk,khd->qhd', weights.astype(jnp.bfloat16), value_heads, pre...  13.5 us
    another operation x8, local copies, waits for them, and re-layouts, attend(): value_heads = value_rows.reshape(value_rows.shape[0], head_count, head_size)  12.5 us
  transfers between devices with their start and end apart: 9, of which 4 were waited for; matrix products, arithmetic and copies ran while one was open for 25% of the time, Pallas kernels for 0%

profile of v1, /device:TPU:10, one launch (start us, length us, event | category | flops | bytes accessed | tf_op | source)
XLA Modules:
  0.0 261.1 jit_solution(7687370874658851220)
XLA Ops:
  1.5 6.3 %all-to-all-start = ((s32[16,1,4,2,8]{4,3,2,1,0:T(2,128)}), s32[16,1,4,2,8]{4,3,2,1,0:T(2,128)S(1)}, u32[]{:S(2)}, u32[]{:S(2)}) async-start(s32[16,1,4,2,8]{4,3,2,1,0:T(2,128)} %stack.91), calls=%async_computation | async-start | bytes 131072 | tf_op jit(solution)/shard_map/all_to_all | solution.py:59
  16.7 4.7 %multiply_reduce_fusion = (f32[20,256]{1,0:T(8,128)S(1)}, f32[20,256,256]{1,2,0:T(8,128)}) fusion(bf16[256,20,128]{0,2,1:T(8,128)(2,1)S(1)} %bitcast.387, bf16[256,20,128]{0,2,1:T(8,128)(2,1)} %bitcast.412), kind=kOutput, calls=%fused_computation.21 | convolution fusion | flops 338160640 | bytes 7884800 | tf_op jit(solution)/shard_map/qhd,khd->hqk/dot_general | solution.py:23
  24.6 3.0 %gather_fusion.2 = bf16[8,32,2560]{2,1,0:T(8,128)(2,1)} fusion(bf16[8,32,2560]{2,1,0:T(8,128)(2,1)} %bitcast.405, s32[1024]{0:T(1024)S(1)} %pad_clamp_fusion.4), kind=kCustom, calls=%fused_computation.4.clone | custom fusion | bytes 2621472 | tf_op jit(solution)/shard_map/jit(_take)/gather | solution.py:75
  29.4 3.0 %gather_fusion = bf16[8,32,2560]{2,1,0:T(8,128)(2,1)} fusion(bf16[8,32,2560]{2,1,0:T(8,128)(2,1)} %bitcast.406, s32[1024]{0:T(1024)S(1)} %pad_clamp_fusion.5), kind=kCustom, calls=%fused_computation.clone | custom fusion | bytes 2621472 | tf_op jit(solution)/shard_map/jit(_take)/gather | solution.py:75
  34.2 2.7 %gather_fusion.6 = bf16[4,32,2560]{2,1,0:T(8,128)(2,1)} fusion(bf16[8,32,2560]{2,1,0:T(8,128)(2,1)} %bitcast.407, s32[1024]{0:T(1024)S(1)} %pad_clamp_fusion.2), kind=kCustom, calls=%fused_computation.7.clone | custom fusion | bytes 1310736 | tf_op jit(solution)/shard_map/jit(_take)/gather | solution.py:75
  41.7 2.6 %gather_fusion.10 = bf16[2,32,2560]{2,1,0:T(8,128)(2,1)} fusion(bf16[8,32,2560]{2,1,0:T(8,128)(2,1)} %bitcast.409, s32[1024]{0:T(1024)S(1)} %pad_clamp_fusion), kind=kCustom, calls=%fused_computation.10.clone | custom fusion | bytes 655368 | tf_op jit(solution)/shard_map/jit(_take)/gather | solution.py:75
  45.7 2.6 %gather_fusion.8 = bf16[2,32,2560]{2,1,0:T(8,128)(2,1)} fusion(bf16[8,32,2560]{2,1,0:T(8,128)(2,1)} %bitcast.410, s32[1024]{0:T(1024)S(1)} %pad_clamp_fusion.1), kind=kCustom, calls=%fused_computation.2.clone | custom fusion | bytes 655368 | tf_op jit(solution)/shard_map/jit(_take)/gather | solution.py:75
  58.0 3.2 %collective-permute-start.1 = (bf16[2,8,32,2560]{3,2,1,0:T(8,128)(2,1)}, bf16[2,8,32,2560]{3,2,1,0:T(8,128)(2,1)}, u32[]{:S(2)}, u32[]{:S(2)}) collective-permute-start(bf16[2,8,32,2560]{3,2,1,0:T(8,128)(2,1)} %pad_maximum_fusion.1), channel_id=1, source_target_pairs={{1,0},{2,1},{3,2},{4,3},{5,4},{6,5},{7,6},{8,7},{9,8},{10,9},{11,1... | collective-permute-start | bytes 7864328 | tf_op jit(solution)/shard_map/ppermute | solution.py:14
  66.7 2.7 %collective-permute-start.3 = (bf16[2,4,32,2560]{3,2,1,0:T(8,128)(2,1)}, bf16[2,4,32,2560]{3,2,1,0:T(8,128)(2,1)}, u32[]{:S(2)}, u32[]{:S(2)}) collective-permute-start(bf16[2,4,32,2560]{3,2,1,0:T(8,128)(2,1)} %pad_maximum_fusion.3), channel_id=1, source_target_pairs={{2,0},{3,1},{4,2},{5,3},{6,4},{7,5},{8,6},{9,7},{10,8},{11,9},{12,... | collective-permute-start | bytes 3932168 | tf_op jit(solution)/shard_map/ppermute | solution.py:14
  70.8 3.3 %collective-permute-start.2 = (bf16[2,4,32,2560]{3,2,1,0:T(8,128)(2,1)}, bf16[2,4,32,2560]{3,2,1,0:T(8,128)(2,1)}, u32[]{:S(2)}, u32[]{:S(2)}) collective-permute-start(bf16[2,4,32,2560]{3,2,1,0:T(8,128)(2,1)} %pad_maximum_fusion.2), channel_id=1, source_target_pairs={{0,2},{1,3},{2,4},{3,5},{4,6},{5,7},{6,8},{7,9},{8,10},{9,11},{10,... | collective-permute-start | bytes 3932168 | tf_op jit(solution)/shard_map/ppermute | solution.py:14
  77.9 54.2 %collective-permute-done.7 = bf16[2,1,32,2560]{3,2,1,0:T(8,128)(2,1)S(1)} collective-permute-done((bf16[2,1,32,2560]{3,2,1,0:T(8,128)(2,1)S(1)}, bf16[2,1,32,2560]{3,2,1,0:T(8,128)(2,1)S(1)}, u32[]{:S(2)}, u32[]{:S(2)}) %collective-permute-start.7) | collective-permute-done | bytes 327712 | tf_op jit(solution)/shard_map/ppermute | solution.py:14
  133.5 4.5 %collective-permute-done.6 = bf16[2,1,32,2560]{3,2,1,0:T(8,128)(2,1)S(1)} collective-permute-done((bf16[2,1,32,2560]{3,2,1,0:T(8,128)(2,1)S(1)}, bf16[2,1,32,2560]{3,2,1,0:T(8,128)(2,1)S(1)}, u32[]{:S(2)}, u32[]{:S(2)}) %collective-permute-start.6) | collective-permute-done | bytes 327712 | tf_op jit(solution)/shard_map/ppermute | solution.py:14
  138.0 16.5 %collective-permute-start.5 = (bf16[2,2,32,2560]{3,2,1,0:T(8,128)(2,1)}, bf16[2,2,32,2560]{3,2,1,0:T(8,128)(2,1)}, u32[]{:S(2)}, u32[]{:S(2)}) collective-permute-start(bf16[2,2,32,2560]{3,2,1,0:T(8,128)(2,1)} %pad_maximum_fusion.5), channel_id=1, source_target_pairs={{4,0},{5,1},{6,2},{7,3},{8,4},{9,5},{10,6},{11,7},{12,8},{13,9},{1... | collective-permute-start | bytes 1966088 | tf_op jit(solution)/shard_map/ppermute | solution.py:14
  158.5 6.9 %collective-permute-done.5 = bf16[2,2,32,2560]{3,2,1,0:T(8,128)(2,1)} collective-permute-done((bf16[2,2,32,2560]{3,2,1,0:T(8,128)(2,1)}, bf16[2,2,32,2560]{3,2,1,0:T(8,128)(2,1)}, u32[]{:S(2)}, u32[]{:S(2)}) %collective-permute-start.5) | collective-permute-done | bytes 655392 | tf_op jit(solution)/shard_map/ppermute | solution.py:14
  165.4 3.9 %collective-permute-start.4 = (bf16[2,2,32,2560]{3,2,1,0:T(8,128)(2,1)S(1)}, bf16[2,2,32,2560]{3,2,1,0:T(8,128)(2,1)}, u32[]{:S(2)}, u32[]{:S(2)}) collective-permute-start(bf16[2,2,32,2560]{3,2,1,0:T(8,128)(2,1)S(1)} %pad_maximum_fusion.4), channel_id=1, source_target_pairs={{0,4},{1,5},{2,6},{3,7},{4,8},{5,9},{6,10},{7,11},{8,12},{9,13},{1... | collective-permute-start | bytes 1966088 | tf_op jit(solution)/shard_map/ppermute | solution.py:14
  171.4 6.6 %collective-permute-done.4 = bf16[2,2,32,2560]{3,2,1,0:T(8,128)(2,1)} collective-permute-done((bf16[2,2,32,2560]{3,2,1,0:T(8,128)(2,1)S(1)}, bf16[2,2,32,2560]{3,2,1,0:T(8,128)(2,1)}, u32[]{:S(2)}, u32[]{:S(2)}) %collective-permute-start.4) | collective-permute-done | bytes 655392 | tf_op jit(solution)/shard_map/ppermute | solution.py:14
  186.0 2.5 fusion.127
  188.5 2.3 reshape_reshape_squeeze.54
  190.8 2.5 fusion.126
  193.3 2.2 reshape_reshape_squeeze.52
  197.8 2.2 reshape_reshape_squeeze.55
  200.0 3.9 %bitcast_reduce_fusion.2 = (f32[20,256]{1,0:T(8,128)}, f32[20,128,256]{2,1,0:T(8,128)}) fusion(pred[128]{0:T(512)(128)(4,1)S(1)} %get-tuple-element.131, bf16[256,20,128]{0,2,1:T(8,128)(2,1)S(1)} %bitcast.392, bf16[128,20,128]{2,1,0:T(8,128)(2,1)} %reshape_reshape_squeeze.54), kind=kOutput, calls=%fused_computation.45 | convolution fusion | flops 169733120 | bytes 4608128 | tf_op jit(solution)/shard_map/qhd,khd->hqk/dot_general | solution.py:23
  205.9 3.5 %fusion.125 = (bf16[1,8,32,2560]{3,2,1,0:T(8,128)(2,1)}, bf16[1,8,32,2560]{3,2,1,0:T(8,128)(2,1)}) fusion(bf16[2,8,32,2560]{3,2,1,0:T(8,128)(2,1)} %collective-permute-done.1), kind=kLoop, calls=%fused_computation.263 | loop fusion | bytes 5242880 | tf_op jit(solution)/shard_map/slice | solution.py:79
  209.4 3.5 %reshape_reshape_squeeze.50 = bf16[256,20,128]{2,1,0:T(8,128)(2,1)} reshape(bf16[1,8,32,2560]{3,2,1,0:T(8,128)(2,1)} %get-tuple-element.53) | data formatting | bytes 2621440 | tf_op jit(solution)/shard_map/reshape;reshape;squeeze | solution.py:21
  212.9 3.5 %fusion.124 = (bf16[1,8,32,2560]{3,2,1,0:T(8,128)(2,1)}, bf16[1,8,32,2560]{3,2,1,0:T(8,128)(2,1)}) fusion(bf16[2,8,32,2560]{3,2,1,0:T(8,128)(2,1)} %collective-permute-done), kind=kLoop, calls=%fused_computation.262 | loop fusion | bytes 5242880 | tf_op jit(solution)/shard_map/slice | solution.py:79
  216.5 3.5 %reshape_reshape_squeeze.48 = bf16[256,20,128]{2,1,0:T(8,128)(2,1)} reshape(bf16[1,8,32,2560]{3,2,1,0:T(8,128)(2,1)} %get-tuple-element.51) | data formatting | bytes 2621440 | tf_op jit(solution)/shard_map/reshape;reshape;squeeze | solution.py:21
  220.0 3.5 %reshape_reshape_squeeze.49 = bf16[256,20,128]{2,1,0:T(8,128)(2,1)} reshape(bf16[1,8,32,2560]{3,2,1,0:T(8,128)(2,1)} %get-tuple-element.50) | data formatting | bytes 2621440 | tf_op jit(solution)/shard_map/reshape;reshape;squeeze | solution.py:22
  223.5 5.2 %bitcast_reduce_fusion = (f32[20,256]{1,0:T(8,128)S(1)}, f32[20,256,256]{1,2,0:T(8,128)}) fusion(pred[256]{0:T(512)(128)(4,1)S(1)} %get-tuple-element.125, bf16[256,20,128]{0,2,1:T(8,128)(2,1)S(1)} %bitcast.394, bf16[256,20,128]{2,1,0:T(8,128)(2,1)} %reshape_reshape_squeeze.50), kind=kOutput, calls=%fused_computation.13 | convolution fusion | flops 339471360 | bytes 7885056 | tf_op jit(solution)/shard_map/qhd,khd->hqk/dot_general | solution.py:23
  231.8 2.5 fusion.4
  234.3 3.0 %fusion.10 = f32[20,128,256]{2,1,0:T(8,128)} fusion(f32[20,256,256]{1,2,0:T(8,128)S(1)} %get-tuple-element.116, f32[20,256]{1,0:T(8,128)S(1)} %get-tuple-element.37, pred[256]{0:T(512)(128)(4,1)S(1)} %copy-done.52, bf16[256,20,128]{2,1,0:T(8,128)(2,1)S(1)} %copy-done.8), kind=kOutput, calls=%fused_computation.29 | convolution fusion | flops 340787200 | bytes 9195776 | tf_op jit(solution)/shard_map/hqk,khd->qhd/dot_general | solution.py:32
  238.9 3.7 %fusion.6 = f32[20,256]{1,0:T(8,128)S(1)} fusion(f32[20,256,256]{1,2,0:T(8,128)} %get-tuple-element.114, f32[20,256]{1,0:T(8,128)} %get-tuple-element.36, pred[256]{0:T(512)(128)(4,1)} %copy-done.50), kind=kLoop, calls=%fused_computation.26 | loop fusion | flops 5237760 | bytes 5284096 | tf_op jit(solution)/shard_map/reduce_sum | solution.py:31
  242.6 3.9 %fusion.8 = f32[20,128,256]{2,1,0:T(8,128)S(1)} fusion(f32[20,256,256]{1,2,0:T(8,128)} %get-tuple-element.114, f32[20,256]{1,0:T(8,128)S(1)} %copy-done.43, pred[256]{0:T(512)(128)(4,1)S(1)} %copy-done.51, bf16[256,20,128]{2,1,0:T(8,128)(2,1)S(1)} %copy-done.9), kind=kOutput, calls=%fused_computation.28 | convolution fusion | flops 340787200 | bytes 9195776 | tf_op jit(solution)/shard_map/hqk,khd->qhd/dot_general | solution.py:32
  (202 shorter events, 78.5 us)
Async XLA Ops:
  0.0 10.9 %copy-start.1 = (bf16[256,2560]{1,0:T(8,128)(2,1)S(1)}, bf16[256,2560]{1,0:T(8,128)(2,1)}, u32[]{:S(2)}) copy-start(bf16[256,2560]{1,0:T(8,128)(2,1)} %param.14) | copy-start | bytes 3932164
  1.5 23.1 %all-to-all-start = ((s32[16,1,4,2,8]{4,3,2,1,0:T(2,128)}), s32[16,1,4,2,8]{4,3,2,1,0:T(2,128)S(1)}, u32[]{:S(2)}, u32[]{:S(2)}) async-start(s32[16,1,4,2,8]{4,3,2,1,0:T(2,128)} %stack.91), calls=%async_computation | async-start | bytes 131072 | tf_op jit(solution)/shard_map/all_to_all | solution.py:59
  14.3 209.2 %copy-start.50 = (pred[256]{0:T(512)(128)(4,1)}, pred[256]{0:T(512)(128)(4,1)S(1)}, u32[]{:S(2)}) copy-start(pred[256]{0:T(512)(128)(4,1)S(1)} %get-tuple-element.125) | copy-start | bytes 772
  16.7 6.4 %copy-start = (bf16[256,2560]{1,0:T(8,128)(2,1)S(1)}, bf16[256,2560]{1,0:T(8,128)(2,1)}, u32[]{:S(2)}) copy-start(bf16[256,2560]{1,0:T(8,128)(2,1)} %param.15) | copy-start | bytes 3932164
  56.3 5.0 %copy-start.11 = (bf16[8,32,2560]{2,1,0:T(8,128)(2,1)S(1)}, bf16[8,32,2560]{2,1,0:T(8,128)(2,1)}, u32[]{:S(2)}) copy-start(bf16[8,32,2560]{2,1,0:T(8,128)(2,1)} %gather_fusion) | copy-start | bytes 3932164
  56.3 5.0 %copy-start.12 = (bf16[8,32,2560]{2,1,0:T(8,128)(2,1)S(1)}, bf16[8,32,2560]{2,1,0:T(8,128)(2,1)}, u32[]{:S(2)}) copy-start(bf16[8,32,2560]{2,1,0:T(8,128)(2,1)} %gather_fusion.1) | copy-start | bytes 3932164
  58.0 147.9 %collective-permute-start.1 = (bf16[2,8,32,2560]{3,2,1,0:T(8,128)(2,1)}, bf16[2,8,32,2560]{3,2,1,0:T(8,128)(2,1)}, u32[]{:S(2)}, u32[]{:S(2)}) collective-permute-start(bf16[2,8,32,2560]{3,2,1,0:T(8,128)(2,1)} %pad_maximum_fusion.1), channel_id=1, source_target_pairs={{1,0},{2,1},{3,2},{4,3},{5,4},{6,5},{7,6},{8,7},{9,8},{10,9},{11,1... | collective-permute-start | bytes 7864328 | tf_op jit(solution)/shard_map/ppermute | solution.py:14
  61.5 3.8 %copy-start.18 = (bf16[4,32,2560]{2,1,0:T(8,128)(2,1)S(1)}, bf16[4,32,2560]{2,1,0:T(8,128)(2,1)}, u32[]{:S(2)}) copy-start(bf16[4,32,2560]{2,1,0:T(8,128)(2,1)} %gather_fusion.6) | copy-start | bytes 1966084
  61.6 3.8 %copy-start.19 = (bf16[4,32,2560]{2,1,0:T(8,128)(2,1)S(1)}, bf16[4,32,2560]{2,1,0:T(8,128)(2,1)}, u32[]{:S(2)}) copy-start(bf16[4,32,2560]{2,1,0:T(8,128)(2,1)} %gather_fusion.7) | copy-start | bytes 1966084
  63.4 149.5 %collective-permute-start = (bf16[2,8,32,2560]{3,2,1,0:T(8,128)(2,1)}, bf16[2,8,32,2560]{3,2,1,0:T(8,128)(2,1)}, u32[]{:S(2)}, u32[]{:S(2)}) collective-permute-start(bf16[2,8,32,2560]{3,2,1,0:T(8,128)(2,1)} %pad_maximum_fusion), channel_id=1, source_target_pairs={{0,1},{1,2},{2,3},{3,4},{4,5},{5,6},{6,7},{7,8},{8,9},{9,10},{10,1... | collective-permute-start | bytes 7864328 | tf_op jit(solution)/shard_map/ppermute | solution.py:14
  65.3 4.1 %copy-start.17 = (bf16[4,32,2560]{2,1,0:T(8,128)(2,1)S(1)}, bf16[4,32,2560]{2,1,0:T(8,128)(2,1)}, u32[]{:S(2)}) copy-start(bf16[4,32,2560]{2,1,0:T(8,128)(2,1)} %gather_fusion.5) | copy-start | bytes 1966084
  66.7 119.3 %collective-permute-start.3 = (bf16[2,4,32,2560]{3,2,1,0:T(8,128)(2,1)}, bf16[2,4,32,2560]{3,2,1,0:T(8,128)(2,1)}, u32[]{:S(2)}, u32[]{:S(2)}) collective-permute-start(bf16[2,4,32,2560]{3,2,1,0:T(8,128)(2,1)} %pad_maximum_fusion.3), channel_id=1, source_target_pairs={{2,0},{3,1},{4,2},{5,3},{6,4},{7,5},{8,6},{9,7},{10,8},{11,9},{12,... | collective-permute-start | bytes 3932168 | tf_op jit(solution)/shard_map/ppermute | solution.py:14
  69.6 6.9 %copy-start.25 = (bf16[2,32,2560]{2,1,0:T(8,128)(2,1)S(1)}, bf16[2,32,2560]{2,1,0:T(8,128)(2,1)}, u32[]{:S(2)}) copy-start(bf16[2,32,2560]{2,1,0:T(8,128)(2,1)} %gather_fusion.10) | copy-start | bytes 983044
  69.6 6.9 %copy-start.26 = (bf16[2,32,2560]{2,1,0:T(8,128)(2,1)S(1)}, bf16[2,32,2560]{2,1,0:T(8,128)(2,1)}, u32[]{:S(2)}) copy-start(bf16[2,32,2560]{2,1,0:T(8,128)(2,1)} %gather_fusion.11) | copy-start | bytes 983044
  70.8 6.8 %copy-start.23 = (bf16[2,32,2560]{2,1,0:T(8,128)(2,1)S(1)}, bf16[2,32,2560]{2,1,0:T(8,128)(2,1)}, u32[]{:S(2)}) copy-start(bf16[2,32,2560]{2,1,0:T(8,128)(2,1)} %gather_fusion.8) | copy-start | bytes 983044
  70.8 6.8 %copy-start.24 = (bf16[2,32,2560]{2,1,0:T(8,128)(2,1)S(1)}, bf16[2,32,2560]{2,1,0:T(8,128)(2,1)}, u32[]{:S(2)}) copy-start(bf16[2,32,2560]{2,1,0:T(8,128)(2,1)} %gather_fusion.9) | copy-start | bytes 983044
  70.8 120.0 %collective-permute-start.2 = (bf16[2,4,32,2560]{3,2,1,0:T(8,128)(2,1)}, bf16[2,4,32,2560]{3,2,1,0:T(8,128)(2,1)}, u32[]{:S(2)}, u32[]{:S(2)}) collective-permute-start(bf16[2,4,32,2560]{3,2,1,0:T(8,128)(2,1)} %pad_maximum_fusion.2), channel_id=1, source_target_pairs={{0,2},{1,3},{2,4},{3,5},{4,6},{5,7},{6,8},{7,9},{8,10},{9,11},{10,... | collective-permute-start | bytes 3932168 | tf_op jit(solution)/shard_map/ppermute | solution.py:14
  75.3 56.8 %collective-permute-start.7 = (bf16[2,1,32,2560]{3,2,1,0:T(8,128)(2,1)S(1)}, bf16[2,1,32,2560]{3,2,1,0:T(8,128)(2,1)S(1)}, u32[]{:S(2)}, u32[]{:S(2)}) collective-permute-start(bf16[2,1,32,2560]{3,2,1,0:T(8,128)(2,1)S(1)} %pad_maximum_fusion.7), channel_id=1, source_target_pairs={{8,0},{9,1},{10,2},{11,3},{12,4},{13,5},{14,6},{15,7},{24,16},{25,... | collective-permute-start | bytes 983048 | tf_op jit(solution)/shard_map/ppermute | solution.py:14
  77.7 78.0 %copy-start.53 = (pred[32]{0:T(512)(128)(4,1)S(1)}, pred[32]{0:T(512)(128)(4,1)}, u32[]{:S(2)}) copy-start(pred[32]{0:T(512)(128)(4,1)} %get-tuple-element.127) | copy-start | bytes 100
  132.0 6.0 %collective-permute-start.6 = (bf16[2,1,32,2560]{3,2,1,0:T(8,128)(2,1)S(1)}, bf16[2,1,32,2560]{3,2,1,0:T(8,128)(2,1)S(1)}, u32[]{:S(2)}, u32[]{:S(2)}) collective-permute-start(bf16[2,1,32,2560]{3,2,1,0:T(8,128)(2,1)S(1)} %pad_maximum_fusion.6), channel_id=1, source_target_pairs={{0,8},{1,9},{2,10},{3,11},{4,12},{5,13},{6,14},{7,15},{16,24},{17,... | collective-permute-start | bytes 983048 | tf_op jit(solution)/shard_map/ppermute | solution.py:14
  138.0 27.3 %collective-permute-start.5 = (bf16[2,2,32,2560]{3,2,1,0:T(8,128)(2,1)}, bf16[2,2,32,2560]{3,2,1,0:T(8,128)(2,1)}, u32[]{:S(2)}, u32[]{:S(2)}) collective-permute-start(bf16[2,2,32,2560]{3,2,1,0:T(8,128)(2,1)} %pad_maximum_fusion.5), channel_id=1, source_target_pairs={{4,0},{5,1},{6,2},{7,3},{8,4},{9,5},{10,6},{11,7},{12,8},{13,9},{1... | collective-permute-start | bytes 1966088 | tf_op jit(solution)/shard_map/ppermute | solution.py:14
  165.4 12.6 %collective-permute-start.4 = (bf16[2,2,32,2560]{3,2,1,0:T(8,128)(2,1)S(1)}, bf16[2,2,32,2560]{3,2,1,0:T(8,128)(2,1)}, u32[]{:S(2)}, u32[]{:S(2)}) collective-permute-start(bf16[2,2,32,2560]{3,2,1,0:T(8,128)(2,1)S(1)} %pad_maximum_fusion.4), channel_id=1, source_target_pairs={{0,4},{1,5},{2,6},{3,7},{4,8},{5,9},{6,10},{7,11},{8,12},{9,13},{1... | collective-permute-start | bytes 1966088 | tf_op jit(solution)/shard_map/ppermute | solution.py:14
  200.0 3.9 %copy-start.16 = (bf16[128,20,128]{2,1,0:T(8,128)(2,1)S(1)}, bf16[128,20,128]{2,1,0:T(8,128)(2,1)}, u32[]{:S(2)}) copy-start(bf16[128,20,128]{2,1,0:T(8,128)(2,1)} %reshape_reshape_squeeze.52) | copy-start | bytes 1966084
  223.5 5.2 %copy-start.7 = (bf16[256,20,128]{2,1,0:T(8,128)(2,1)S(1)}, bf16[256,20,128]{2,1,0:T(8,128)(2,1)}, u32[]{:S(2)}) copy-start(bf16[256,20,128]{2,1,0:T(8,128)(2,1)} %reshape_reshape_squeeze.48) | copy-start | bytes 3932164
  223.5 5.2 %copy-start.52 = (pred[256]{0:T(512)(128)(4,1)S(1)}, pred[256]{0:T(512)(128)(4,1)}, u32[]{:S(2)}) copy-start(pred[256]{0:T(512)(128)(4,1)} %get-tuple-element.126) | copy-start | bytes 772
  234.2 3.0 %copy-start.10 = (bf16[1,8,32,2560]{3,2,1,0:T(8,128)(2,1)S(1)}, bf16[1,8,32,2560]{3,2,1,0:T(8,128)(2,1)}, u32[]{:S(2)}) copy-start(bf16[1,8,32,2560]{3,2,1,0:T(8,128)(2,1)} %get-tuple-element.52) | copy-start | bytes 3932164
  238.9 3.7 %copy-start.9 = (bf16[256,20,128]{2,1,0:T(8,128)(2,1)S(1)}, bf16[256,20,128]{2,1,0:T(8,128)(2,1)}, u32[]{:S(2)}) copy-start(bf16[256,20,128]{2,1,0:T(8,128)(2,1)} %reshape_reshape_squeeze.51) | copy-start | bytes 3932164
  238.9 3.7 %copy-start.43 = (f32[20,256]{1,0:T(8,128)S(1)}, f32[20,256]{1,0:T(8,128)}, u32[]{:S(2)}) copy-start(f32[20,256]{1,0:T(8,128)} %get-tuple-element.36) | copy-start | bytes 61444
  238.9 3.7 %copy-start.51 = (pred[256]{0:T(512)(128)(4,1)S(1)}, pred[256]{0:T(512)(128)(4,1)}, u32[]{:S(2)}) copy-start(pred[256]{0:T(512)(128)(4,1)} %copy-done.50) | copy-start | bytes 772
  242.6 4.0 %copy-start.3 = (f32[20,128,256]{2,1,0:T(8,128)S(1)}, f32[20,128,256]{2,1,0:T(8,128)}, u32[]{:S(2)}) copy-start(f32[20,128,256]{2,1,0:T(8,128)} %get-tuple-element.112) | copy-start | bytes 7864324
  242.6 4.0 %copy-start.29 = (f32[20,256]{1,0:T(8,128)S(1)}, f32[20,256]{1,0:T(8,128)}, u32[]{:S(2)}) copy-start(f32[20,256]{1,0:T(8,128)} %get-tuple-element.35) | copy-start | bytes 61444
  247.7 3.2 %slice-start = ((s8[5242880]{0:T(1024)(128)(4,1)}), s8[4194304]{0:T(1024)(128)(4,1)S(1)}, s32[]{:S(2)}) async-start(s8[5242880]{0:T(1024)(128)(4,1)} %bitcast.396), calls=%async_computation.1 | async-start | bytes 8388608
  (33 other events, 48.7 us)
